TPU v7x, 32 devices: a whole 2x2x4 slice. The times are simulated.
32 devices in a mesh: grp: 4 (over y, core), dev: 8 (over z, x).
Axes of the slice: x: 2, y: 2, z: 4, core: 2. Of those that a mesh axis runs over, the one named last changes fastest.
Arguments:
- centers: bfloat16 [4096, 128], P(('grp', 'dev')), may hold values from -4 to 4
- center_weights: bfloat16 [4096, 64], P(('grp', 'dev')), may hold values from -0.75 to 0.75
- batch: bfloat16 [8192, 128], P('dev'), may hold values from -4 to 4
- labels: bfloat16 [8192, 64], P('dev'), may hold values from -6 to 6
- sub_centers: bfloat16 [2048, 128], P('grp'), may hold values from -4 to 4
- eig_vectors: bfloat16 [2048, 160], P('grp'), may hold values from -0.5 to 0.5
- eig_scale: float32 [160], replicated, may hold values from 0.02 to 0.4
Outputs:
- predictions: float32 [8192, 64], P('dev')
- center_step: float32 [4096, 64], P(('grp', 'dev'))
- nystrom_fix: float32 [2048, 64], P('grp')
All inputs are finite; a program needn't handle non-finite values.
Results may differ from a plain program's by a relative error of at most 0.0031.
Values may be sent and summed in bfloat16 or wider, within the bound.
A program may use at most 64 MiB of HBM per device.

v0:
```python
import math
import jax
import jax.numpy as jnp
from jax import lax
from jax.sharding import PartitionSpec as P

gamma_scale = 0.25
learn_rate = 8.0


def sq_norms(points):
    return jnp.sum(jnp.square(points.astype(jnp.float32)), axis=1)


def kernel_tile(left, left_sq, right, right_sq):
    cross = lax.dot_general(
        left, right, (((1,), (1,)), ((), ())), preferred_element_type=jnp.float32
    )
    dist = left_sq[:, None] + right_sq[None, :] - 2.0 * cross
    return jnp.exp(-gamma_scale * dist).astype(jnp.bfloat16)


def body(centers, center_weights, batch, labels, sub_centers, eig_vectors, eig_scale):
    samples = batch.shape[0]
    width_in = batch.shape[1]
    width_out = labels.shape[1]
    block = min(512, samples)
    num_blocks = samples // block
    factor = learn_rate / math.sqrt(samples * lax.axis_size("dev"))
    batch_sq = sq_norms(batch)
    batch_blocks = batch.reshape(num_blocks, block, width_in)
    sq_blocks = batch_sq.reshape(num_blocks, block)
    group_centers, group_weights = (
        lax.all_gather(centers, "dev", axis=0, tiled=True),
        lax.all_gather(center_weights, "dev", axis=0, tiled=True),
    )
    group_sq = sq_norms(group_centers)

    def pred_rows(inputs):
        rows_x, rows_sq = inputs
        tile = kernel_tile(rows_x, rows_sq, group_centers, group_sq)
        return jnp.dot(tile, group_weights, preferred_element_type=jnp.float32)

    partial_pred = lax.map(pred_rows, (batch_blocks, sq_blocks)).reshape(samples, width_out)
    predictions = lax.psum(partial_pred, "grp")
    resid = (predictions - labels.astype(jnp.float32)).astype(jnp.bfloat16)
    resid_blocks = resid.reshape(num_blocks, block, width_out)
    rows_sq = group_sq

    def add_block(accum, inputs):
        rows_x, part_sq, rows_r = inputs
        tile = kernel_tile(group_centers, rows_sq, rows_x, part_sq)
        return (accum + jnp.dot(tile, rows_r, preferred_element_type=jnp.float32), None)

    result, _ = lax.scan(
        add_block,
        jnp.zeros((lax.axis_size("dev") * centers.shape[0], width_out), jnp.float32),
        (batch_blocks, sq_blocks, resid_blocks),
    )
    center_step = lax.psum_scatter(result, "dev", scatter_dimension=0, tiled=True) * factor
    sub_sq = sq_norms(sub_centers)

    def sub_block(accum, inputs):
        rows_x, rows_sq, rows_r = inputs
        tile = kernel_tile(sub_centers, sub_sq, rows_x, rows_sq)
        return (accum + jnp.dot(tile, rows_r, preferred_element_type=jnp.float32), None)

    sub_part, _ = lax.scan(
        sub_block,
        jnp.zeros((sub_centers.shape[0], width_out), jnp.float32),
        (batch_blocks, sq_blocks, resid_blocks),
    )
    sub_part = sub_part * factor
    vectors = eig_vectors.astype(jnp.float32)
    dims = (((0,), (0,)), ((), ()))
    proj_part = lax.dot_general(vectors, sub_part, dims, precision=lax.Precision.HIGHEST)
    proj = lax.psum(proj_part, ("grp", "dev"))
    nystrom_fix = jnp.dot(vectors, eig_scale[:, None] * proj, precision=lax.Precision.HIGHEST)
    return (predictions, center_step, nystrom_fix)


def solution(mesh):
    placed = (
        P(("grp", "dev"), None),
        P(("grp", "dev"), None),
        P("dev", None),
        P("dev", None),
        P("grp", None),
        P("grp", None),
        P(),
    )
    return jax.shard_map(
        body,
        mesh=mesh,
        in_specs=placed,
        out_specs=(P("dev", None), P(("grp", "dev"), None), P("grp", None)),
        check_vma=False,
    )
```

profile of v0, /device:TPU:0, one launch (start us, length us, event | category | flops | bytes accessed | tf_op | source)
XLA Modules:
  0.0 186.0 jit_solution(1019431074230919624)
XLA Ops:
  7.2 0.0 copy-start
  7.2 0.0 all-reduce.2.cloned.1.call-start
  7.2 0.0 copy-start.2
  7.2 32.9 %all_gather.6 = bf16[1024,128]{1,0:T(8,128)(2,1)S(1)} all-gather(bf16[128,128]{1,0:T(8,128)(2,1)} %param.13), channel_id=1, replica_groups=mesh['grp'=4,'dev'=8] {'dev'}, dimensions={0}, use_global_device_ids=true | all-gather | bytes 294912 | tf_op jit(solution)/shard_map/all_gather | solution.py:34
  40.1 0.0 copy-start.6
  40.1 0.2 multiply_reduce_fusion
  40.4 0.0 copy-done.2
  40.4 0.2 multiply_reduce_fusion.1
  40.6 0.3 copy-done.6
  40.9 0.1 copy.10
  41.0 30.7 %all_gather.7 = bf16[1024,64]{1,0:T(8,128)(2,1)S(1)} all-gather(bf16[128,64]{1,0:T(8,128)(2,1)S(1)} %copy.10), channel_id=1, replica_groups=mesh['grp'=4,'dev'=8] {'dev'}, dimensions={0}, use_global_device_ids=true | all-gather | bytes 147456 | tf_op jit(solution)/shard_map/all_gather | solution.py:35
  71.7 4.5 %while.32 = (s32[]{:T(128)}, f32[2,512,64]{1,0,2:T(2,128)S(1)}, f32[2,512]{1,0:T(2,128)S(1)}, f32[1024]{0:T(1024)S(1)}, bf16[2,512,128]{2,1,0:T(8,128)(2,1)S(1)}...) while((s32[]{:T(128)}, f32[2,512,64]{1,0,2:T(2,128)S(1)}, ...), condition=%wide.region_3.4_spmd, body=%wide.region_2.3_spmd.sunk | while | flops 203948032 | bytes 1321065 | solution.py:44
  71.7 0.9 fusion.81
  72.6 0.1 copy.22
  72.7 1.2 dynamic_update_slice.5
  74.0 0.9 fusion.81
  74.9 0.1 copy.22
  75.0 1.2 dynamic_update_slice.5
  76.2 0.8 copy.20
  77.0 0.0 copy-start.5
  77.0 0.0 all-reduce.2.cloned.1.call-update
  77.0 0.0 reduce-scatter.2.cloned.1.call-start
  77.1 0.8 copy-done.4
  77.9 0.1 multiply_reduce_fusion.2
  78.0 32.6 %all-reduce.2.cloned.1.call-done = f32[1024,64]{0,1:T(8,128)} async-done(((f32[1024,64]{0,1:T(8,128)}), f32[1024,64]{0,1:T(8,128)}) %all-reduce.2.cloned.1.call-update) | async-done | bytes 262160 | tf_op jit(solution)/shard_map/psum | solution.py:45
  110.6 0.0 copy-done.5
  110.6 1.0 subtract_convert_fusion
  111.6 0.2 copy.14
  111.8 1.8 while.33
  111.8 0.9 fusion.85
  112.7 0.9 fusion.85
  113.6 0.0 copy-start.3
  113.6 0.7 copy-done.3
  114.3 0.0 reduce-scatter.2.cloned.1.call-update
  114.3 1.3 while.34
  114.3 0.6 fusion.89
  115.0 0.6 fusion.89
  115.6 0.0 copy-done
  115.6 0.0 copy-start.7
  115.6 0.3 convolution_bitcast_fusion.1
  115.9 40.1 %psum.15 = f32[160,64]{1,0:T(8,128)S(1)} all-reduce(f32[160,64]{1,0:T(8,128)S(1)} %convolution_bitcast_fusion.1), channel_id=1, replica_groups=mesh['grp'=4,'dev'=8] {'grp','dev'}, use_global_device_ids=true, to_apply=%region_11.12 | all-reduce | flops 10240 | bytes 81920 | tf_op jit(solution)/shard_map/psum | solution.py:77
  156.0 0.0 copy-done.7
  156.0 0.0 copy-start.1
  156.0 1.0 convolution_bitcast_fusion
  157.0 20.0 %reduce-scatter.2.cloned.1.call-done = f32[128,64]{0,1:T(8,128)} async-done(((f32[1024,64]{0,1:T(8,128)}), f32[128,64]{0,1:T(8,128)}) %reduce-scatter.2.cloned.1.call-update) | async-done | bytes 32784 | tf_op jit(solution)/shard_map/reduce_scatter | solution.py:60
  177.0 1.4 broadcast_multiply_fusion
  178.4 0.0 copy-done.1
  178.4 0.7 copy.43
  (11 shorter events, 0.1 us)
Async XLA Ops:
  7.2 108.4 %copy-start = (bf16[512,160]{0,1:T(8,128)(2,1)S(1)}, bf16[512,160]{0,1:T(8,128)(2,1)}, u32[]{:S(2)}) copy-start(bf16[512,160]{0,1:T(8,128)(2,1)} %param.18) | copy-start | bytes 491524
  7.2 103.4 %all-reduce.2.cloned.1.call-start = ((), (), s32[]{:S(2)}) async-start(), calls=%async_computation.1 | async-start | bytes 524288 | tf_op jit(solution)/shard_map/psum | solution.py:45
  7.2 33.1 %copy-start.2 = (bf16[1024,128]{1,0:T(8,128)(2,1)S(1)}, bf16[1024,128]{1,0:T(8,128)(2,1)}, u32[]{:S(2)}) copy-start(bf16[1024,128]{1,0:T(8,128)(2,1)} %param.15) | copy-start | bytes 786436
  40.1 0.7 copy-start.6
  77.0 0.9 copy-start.4
  77.0 33.6 %copy-start.5 = (bf16[1024,64]{0,1:T(8,128)(2,1)S(1)}, bf16[1024,64]{0,1:T(8,128)(2,1)}, u32[]{:S(2)}) copy-start(bf16[1024,64]{0,1:T(8,128)(2,1)} %param.16) | copy-start | bytes 393220
  77.0 100.0 %reduce-scatter.2.cloned.1.call-start = ((), (), s32[]{:S(2)}) async-start(), calls=%async_computation.2 | async-start | bytes 294912 | tf_op jit(solution)/shard_map/reduce_scatter | solution.py:60
  113.6 0.7 copy-start.3
  115.6 40.4 %copy-start.7 = (f32[160]{0:T(256)S(1)}, f32[160]{0:T(256)}, u32[]{:S(2)}) copy-start(f32[160]{0:T(256)} %param.19) | copy-start | bytes 1924
  156.0 22.4 %copy-start.1 = (f32[1024,64]{0,1:T(8,128)S(1)}, f32[1024,64]{0,1:T(8,128)}, u32[]{:S(2)}) copy-start(f32[1024,64]{0,1:T(8,128)} %all-reduce.2.cloned.1.call-done) | copy-start | bytes 786436
Sparse Core Ops, SparseCore 0:
  77.1 33.4 all-reduce.1
  114.5 62.5 reduce-scatter.1
where the time goes:
time: 186 us
  blocking collectives  104 us (56%)
  waiting for transfers between devices  52.6 us (28%)
  between operations  14.2 us (8%)
  local copies, waits for them, and re-layouts  6.28 us (3%)
  matrix products  5.97 us (3%)
  other arithmetic  2.92 us (2%)
    psum x1, blocking collectives, body(): proj = lax.psum(proj_part, ('grp', 'dev'))  40.1 us
    all_gather x1, blocking collectives, body(): lax.all_gather(centers, 'dev', axis=0, tiled=True)  32.9 us
    psum x1, waiting for transfers between devices, body(): predictions = lax.psum(partial_pred, 'grp')  32.6 us
    all_gather x1, blocking collectives, body(): lax.all_gather(center_weights, 'dev', axis=0, tiled=True)  30.7 us
    reduce_scatter x1, waiting for transfers between devices, body(): lax.psum_scatter(result, 'dev', scatter_dimension=0, tiled=True) * factor  20 us
  transfers between devices with their start and end apart: 2, of which 2 were waited for; matrix products, arithmetic and copies ran while one was open for 1% of the time, Pallas kernels for 0%

commit v1 on v0

--- a/solution.py
+++ b/solution.py
@@ -1,3 +1,4 @@
+import functools
 import math
 import jax
 import jax.numpy as jnp
@@ -6,6 +7,24 @@
 
 gamma_scale = 0.25
 learn_rate = 8.0
+
+
+def runs_note(vector, which_dim):
+    parts_n = lax.axis_size("dev")
+    arrivals = [vector]
+    for no in range(1, parts_n):
+        arrivals.append(
+            lax.ppermute(
+                arrivals[no - 1], "dev", [(dd, (dd - 1) % parts_n) for dd in range(parts_n)]
+            )
+        )
+    current_value = jnp.concatenate(arrivals, axis=which_dim)
+    return jnp.roll(
+        current_value, shift=lax.axis_index("dev") * vector.shape[which_dim], axis=which_dim
+    )
+
+
+guide_entries = functools.partial(runs_note, which_dim=0)
 
 
 def sq_norms(points):
@@ -32,7 +51,7 @@
     sq_blocks = batch_sq.reshape(num_blocks, block)
     group_centers, group_weights = (
         lax.all_gather(centers, "dev", axis=0, tiled=True),
-        lax.all_gather(center_weights, "dev", axis=0, tiled=True),
+        guide_entries(center_weights),
     )
     group_sq = sq_norms(group_centers)
 

time: 186 us -> 196 us (1.054)
  blocking collectives: 104 us -> 71 us
  starting transfers between devices: 0.08 us -> 30 us
  waiting for transfers between devices: 52.6 us -> 65.4 us
    all_gather x1 -> x0, blocking collectives: 30.7 us -> none  [body(): lax.all_gather(center_weights, 'dev', axis=0, tiled=True)]
    ppermute x0 -> x7, starting transfers between devices: none -> 29.9 us  [runs_note(): lax.ppermute(arrivals[no - 1], 'dev', [(dd, (dd - 1) % parts_n) for dd in...]
    ppermute x0 -> x7, waiting for transfers between devices: none -> 11.5 us  [runs_note(): lax.ppermute(arrivals[no - 1], 'dev', [(dd, (dd - 1) % parts_n) for dd in...]
  transfers between devices with their start and end apart: 2 -> 9, of which waited for: 2 -> 8; matrix products, arithmetic and copies ran while one was open for 1% -> 2% of each run, Pallas kernels for 0% -> 0%
where the time goes in v1:
time: 196 us
  blocking collectives  71 us (36%)
  waiting for transfers between devices  65.4 us (33%)
  starting transfers between devices  30 us (15%)
  between operations  14.3 us (7%)
  local copies, waits for them, and re-layouts  6.19 us (3%)
  matrix products  5.98 us (3%)
  other arithmetic  2.92 us (1%)
    psum x1, blocking collectives, body(): proj = lax.psum(proj_part, ('grp', 'dev'))  40.1 us
    psum x1, waiting for transfers between devices, body(): predictions = lax.psum(partial_pred, 'grp')  33.9 us
    all_gather x1, blocking collectives, body(): lax.all_gather(centers, 'dev', axis=0, tiled=True)  31 us
    ppermute x7, starting transfers between devices, runs_note(): lax.ppermute(arrivals[no - 1], 'dev', [(dd, (dd - 1) % parts_n) for dd in...  29.9 us
    reduce_scatter x1, waiting for transfers between devices, body(): lax.psum_scatter(result, 'dev', scatter_dimension=0, tiled=True) * factor  20 us
    ppermute x7, waiting for transfers between devices, runs_note(): lax.ppermute(arrivals[no - 1], 'dev', [(dd, (dd - 1) % parts_n) for dd in...  11.5 us
  transfers between devices with their start and end apart: 9, of which 8 were waited for; matrix products, arithmetic and copies ran while one was open for 2% of the time, Pallas kernels for 0%

profile of v1, /device:TPU:0, one launch (start us, length us, event | category | flops | bytes accessed | tf_op | source)
XLA Modules:
  0.0 196.0 jit_solution(5597858175779662054)
XLA Ops:
  7.2 0.0 copy-start
  7.2 0.0 all-reduce.2.cloned.1.call-start
  7.2 0.9 copy.11
  8.1 6.1 %collective-permute-start = (bf16[128,64]{1,0:T(8,128)(2,1)S(1)}, bf16[128,64]{1,0:T(8,128)(2,1)S(1)}, u32[]{:S(2)}, u32[]{:S(2)}) collective-permute-start(bf16[128,64]{1,0:T(8,128)(2,1)S(1)} %copy.11), channel_id=1, source_target_pairs={{0,7},{1,0},{2,1},{3,2},{4,3},{5,4},{6,5},{7,6},{8,15},{9,8},{10,9... | collective-permute-start | bytes 49160 | tf_op jit(solution)/shard_map/ppermute | solution.py:17
  14.2 31.0 %all_gather.3 = bf16[1024,128]{1,0:T(8,128)(2,1)S(1)} all-gather(bf16[128,128]{1,0:T(8,128)(2,1)} %param.13), channel_id=1, replica_groups=mesh['grp'=4,'dev'=8] {'dev'}, dimensions={0}, use_global_device_ids=true | all-gather | bytes 294912 | tf_op jit(solution)/shard_map/all_gather | solution.py:53
  45.1 0.2 multiply_reduce_fusion
  45.4 0.2 multiply_reduce_fusion.1
  45.6 0.7 collective-permute-start.1
  46.4 3.5 %collective-permute-done.1 = bf16[128,64]{1,0:T(8,128)(2,1)S(1)} collective-permute-done((bf16[128,64]{1,0:T(8,128)(2,1)S(1)}, bf16[128,64]{1,0:T(8,128)(2,1)S(1)}, u32[]{:S(2)}, u32[]{:S(2)}) %collective-permute-start.1) | collective-permute-done | bytes 16416 | tf_op jit(solution)/shard_map/ppermute | solution.py:17
  49.9 3.1 %collective-permute-start.2 = (bf16[128,64]{1,0:T(8,128)(2,1)S(1)}, bf16[128,64]{1,0:T(8,128)(2,1)S(1)}, u32[]{:S(2)}, u32[]{:S(2)}) collective-permute-start(bf16[128,64]{1,0:T(8,128)(2,1)S(1)} %collective-permute-done.1), channel_id=1, source_target_pairs={{0,7},{1,0},{2,1},{3,2},{4,3},{5,4},{6,5},{7,6},{8,15},{9,8},{10,9... | collective-permute-start | bytes 49160 | tf_op jit(solution)/shard_map/ppermute | solution.py:17
  53.0 1.6 collective-permute-done.2
  54.6 5.0 %collective-permute-start.3 = (bf16[128,64]{1,0:T(8,128)(2,1)S(1)}, bf16[128,64]{1,0:T(8,128)(2,1)S(1)}, u32[]{:S(2)}, u32[]{:S(2)}) collective-permute-start(bf16[128,64]{1,0:T(8,128)(2,1)S(1)} %collective-permute-done.2), channel_id=1, source_target_pairs={{0,7},{1,0},{2,1},{3,2},{4,3},{5,4},{6,5},{7,6},{8,15},{9,8},{10,9... | collective-permute-start | bytes 49160 | tf_op jit(solution)/shard_map/ppermute | solution.py:17
  59.6 1.6 collective-permute-done.3
  61.2 5.0 %collective-permute-start.4 = (bf16[128,64]{1,0:T(8,128)(2,1)S(1)}, bf16[128,64]{1,0:T(8,128)(2,1)S(1)}, u32[]{:S(2)}, u32[]{:S(2)}) collective-permute-start(bf16[128,64]{1,0:T(8,128)(2,1)S(1)} %collective-permute-done.3), channel_id=1, source_target_pairs={{0,7},{1,0},{2,1},{3,2},{4,3},{5,4},{6,5},{7,6},{8,15},{9,8},{10,9... | collective-permute-start | bytes 49160 | tf_op jit(solution)/shard_map/ppermute | solution.py:17
  66.2 1.6 collective-permute-done.4
  67.8 5.0 %collective-permute-start.5 = (bf16[128,64]{1,0:T(8,128)(2,1)S(1)}, bf16[128,64]{1,0:T(8,128)(2,1)S(1)}, u32[]{:S(2)}, u32[]{:S(2)}) collective-permute-start(bf16[128,64]{1,0:T(8,128)(2,1)S(1)} %collective-permute-done.4), channel_id=1, source_target_pairs={{0,7},{1,0},{2,1},{3,2},{4,3},{5,4},{6,5},{7,6},{8,15},{9,8},{10,9... | collective-permute-start | bytes 49160 | tf_op jit(solution)/shard_map/ppermute | solution.py:17
  72.8 1.6 collective-permute-done.5
  74.4 5.0 %collective-permute-start.6 = (bf16[128,64]{1,0:T(8,128)(2,1)S(1)}, bf16[128,64]{1,0:T(8,128)(2,1)S(1)}, u32[]{:S(2)}, u32[]{:S(2)}) collective-permute-start(bf16[128,64]{1,0:T(8,128)(2,1)S(1)} %collective-permute-done.5), channel_id=1, source_target_pairs={{0,7},{1,0},{2,1},{3,2},{4,3},{5,4},{6,5},{7,6},{8,15},{9,8},{10,9... | collective-permute-start | bytes 49160 | tf_op jit(solution)/shard_map/ppermute | solution.py:17
  79.5 1.6 collective-permute-done.6
  81.2 4.5 %while.32 = (s32[]{:T(128)}, f32[2,512,64]{1,0,2:T(2,128)S(1)}, f32[2,512]{1,0:T(2,128)S(1)}, f32[1024]{0:T(1024)S(1)}, bf16[2,512,128]{2,1,0:T(8,128)(2,1)S(1)}...) while((s32[]{:T(128)}, f32[2,512,64]{1,0,2:T(2,128)S(1)}, ...), condition=%wide.region_3.4_spmd, body=%wide.region_2.3_spmd.sunk | while | flops 203948032 | bytes 1321065 | solution.py:63
  81.2 0.9 fusion.81
  82.1 0.1 copy.24
  82.2 1.2 dynamic_update_slice.5
  83.5 0.9 fusion.81
  84.4 0.1 copy.24
  84.5 1.2 dynamic_update_slice.5
  85.8 0.8 copy.22
  86.5 0.0 all-reduce.2.cloned.1.call-update
  86.5 0.0 reduce-scatter.2.cloned.1.call-start
  86.6 0.0 copy-done.4
  86.6 0.1 multiply_reduce_fusion.2
  86.8 33.9 %all-reduce.2.cloned.1.call-done = f32[1024,64]{0,1:T(8,128)} async-done(((f32[1024,64]{0,1:T(8,128)}), f32[1024,64]{0,1:T(8,128)}) %all-reduce.2.cloned.1.call-update) | async-done | bytes 262160 | tf_op jit(solution)/shard_map/psum | solution.py:64
  120.7 1.0 subtract_convert_fusion
  121.7 0.2 copy.16
  121.9 1.8 while.33
  121.9 0.9 fusion.85
  122.8 0.9 fusion.85
  123.7 0.7 copy-done.3
  124.4 0.0 reduce-scatter.2.cloned.1.call-update
  124.4 1.3 while.34
  124.5 0.6 fusion.89
  125.1 0.6 fusion.89
  125.7 0.3 convolution_bitcast_fusion.1
  126.0 40.1 %psum.15 = f32[160,64]{1,0:T(8,128)S(1)} all-reduce(f32[160,64]{1,0:T(8,128)S(1)} %convolution_bitcast_fusion.1), channel_id=1, replica_groups=mesh['grp'=4,'dev'=8] {'grp','dev'}, use_global_device_ids=true, to_apply=%region_11.12 | all-reduce | flops 10240 | bytes 81920 | tf_op jit(solution)/shard_map/psum | solution.py:96
  166.1 1.0 convolution_bitcast_fusion
  167.1 20.0 %reduce-scatter.2.cloned.1.call-done = f32[128,64]{0,1:T(8,128)} async-done(((f32[1024,64]{0,1:T(8,128)}), f32[128,64]{0,1:T(8,128)}) %reduce-scatter.2.cloned.1.call-update) | async-done | bytes 32784 | tf_op jit(solution)/shard_map/reduce_scatter | solution.py:79
  187.1 1.4 broadcast_multiply_fusion
  188.5 0.7 copy.60
  (39 shorter events, 0.3 us)
Async XLA Ops:
  7.2 118.6 %copy-start = (bf16[512,160]{0,1:T(8,128)(2,1)S(1)}, bf16[512,160]{0,1:T(8,128)(2,1)}, u32[]{:S(2)}) copy-start(bf16[512,160]{0,1:T(8,128)(2,1)} %param.18) | copy-start | bytes 491524
  7.2 38.2 %copy-start.2 = (bf16[1024,128]{1,0:T(8,128)(2,1)S(1)}, bf16[1024,128]{1,0:T(8,128)(2,1)}, u32[]{:S(2)}) copy-start(bf16[1024,128]{1,0:T(8,128)(2,1)} %param.15) | copy-start | bytes 786436
  7.2 113.5 %all-reduce.2.cloned.1.call-start = ((), (), s32[]{:S(2)}) async-start(), calls=%async_computation.1 | async-start | bytes 524288 | tf_op jit(solution)/shard_map/psum | solution.py:64
  8.1 37.5 %collective-permute-start = (bf16[128,64]{1,0:T(8,128)(2,1)S(1)}, bf16[128,64]{1,0:T(8,128)(2,1)S(1)}, u32[]{:S(2)}, u32[]{:S(2)}) collective-permute-start(bf16[128,64]{1,0:T(8,128)(2,1)S(1)} %copy.11), channel_id=1, source_target_pairs={{0,7},{1,0},{2,1},{3,2},{4,3},{5,4},{6,5},{7,6},{8,15},{9,8},{10,9... | collective-permute-start | bytes 49160 | tf_op jit(solution)/shard_map/ppermute | solution.py:17
  45.6 4.3 %collective-permute-start.1 = (bf16[128,64]{1,0:T(8,128)(2,1)S(1)}, bf16[128,64]{1,0:T(8,128)(2,1)S(1)}, u32[]{:S(2)}, u32[]{:S(2)}) collective-permute-start(bf16[128,64]{1,0:T(8,128)(2,1)S(1)} %collective-permute-done), channel_id=1, source_target_pairs={{0,7},{1,0},{2,1},{3,2},{4,3},{5,4},{6,5},{7,6},{8,15},{9,8},{10,9... | collective-permute-start | bytes 49160 | tf_op jit(solution)/shard_map/ppermute | solution.py:17
  49.9 4.7 %collective-permute-start.2 = (bf16[128,64]{1,0:T(8,128)(2,1)S(1)}, bf16[128,64]{1,0:T(8,128)(2,1)S(1)}, u32[]{:S(2)}, u32[]{:S(2)}) collective-permute-start(bf16[128,64]{1,0:T(8,128)(2,1)S(1)} %collective-permute-done.1), channel_id=1, source_target_pairs={{0,7},{1,0},{2,1},{3,2},{4,3},{5,4},{6,5},{7,6},{8,15},{9,8},{10,9... | collective-permute-start | bytes 49160 | tf_op jit(solution)/shard_map/ppermute | solution.py:17
  54.6 6.6 %collective-permute-start.3 = (bf16[128,64]{1,0:T(8,128)(2,1)S(1)}, bf16[128,64]{1,0:T(8,128)(2,1)S(1)}, u32[]{:S(2)}, u32[]{:S(2)}) collective-permute-start(bf16[128,64]{1,0:T(8,128)(2,1)S(1)} %collective-permute-done.2), channel_id=1, source_target_pairs={{0,7},{1,0},{2,1},{3,2},{4,3},{5,4},{6,5},{7,6},{8,15},{9,8},{10,9... | collective-permute-start | bytes 49160 | tf_op jit(solution)/shard_map/ppermute | solution.py:17
  61.2 6.6 %collective-permute-start.4 = (bf16[128,64]{1,0:T(8,128)(2,1)S(1)}, bf16[128,64]{1,0:T(8,128)(2,1)S(1)}, u32[]{:S(2)}, u32[]{:S(2)}) collective-permute-start(bf16[128,64]{1,0:T(8,128)(2,1)S(1)} %collective-permute-done.3), channel_id=1, source_target_pairs={{0,7},{1,0},{2,1},{3,2},{4,3},{5,4},{6,5},{7,6},{8,15},{9,8},{10,9... | collective-permute-start | bytes 49160 | tf_op jit(solution)/shard_map/ppermute | solution.py:17
  67.8 6.6 %collective-permute-start.5 = (bf16[128,64]{1,0:T(8,128)(2,1)S(1)}, bf16[128,64]{1,0:T(8,128)(2,1)S(1)}, u32[]{:S(2)}, u32[]{:S(2)}) collective-permute-start(bf16[128,64]{1,0:T(8,128)(2,1)S(1)} %collective-permute-done.4), channel_id=1, source_target_pairs={{0,7},{1,0},{2,1},{3,2},{4,3},{5,4},{6,5},{7,6},{8,15},{9,8},{10,9... | collective-permute-start | bytes 49160 | tf_op jit(solution)/shard_map/ppermute | solution.py:17
  74.4 6.6 %collective-permute-start.6 = (bf16[128,64]{1,0:T(8,128)(2,1)S(1)}, bf16[128,64]{1,0:T(8,128)(2,1)S(1)}, u32[]{:S(2)}, u32[]{:S(2)}) collective-permute-start(bf16[128,64]{1,0:T(8,128)(2,1)S(1)} %collective-permute-done.5), channel_id=1, source_target_pairs={{0,7},{1,0},{2,1},{3,2},{4,3},{5,4},{6,5},{7,6},{8,15},{9,8},{10,9... | collective-permute-start | bytes 49160 | tf_op jit(solution)/shard_map/ppermute | solution.py:17
  85.7 0.9 copy-start.4
  85.7 35.0 %copy-start.5 = (bf16[1024,64]{0,1:T(8,128)(2,1)S(1)}, bf16[1024,64]{0,1:T(8,128)(2,1)}, u32[]{:S(2)}) copy-start(bf16[1024,64]{0,1:T(8,128)(2,1)} %param.16) | copy-start | bytes 393220
  86.5 100.6 %reduce-scatter.2.cloned.1.call-start = ((), (), s32[]{:S(2)}) async-start(), calls=%async_computation.2 | async-start | bytes 294912 | tf_op jit(solution)/shard_map/reduce_scatter | solution.py:79
  123.7 0.7 copy-start.3
  125.7 40.4 %copy-start.6 = (f32[160]{0:T(256)S(1)}, f32[160]{0:T(256)}, u32[]{:S(2)}) copy-start(f32[160]{0:T(256)} %param.19) | copy-start | bytes 1924
  125.7 62.7 %copy-start.1 = (f32[1024,64]{0,1:T(8,128)S(1)}, f32[1024,64]{0,1:T(8,128)}, u32[]{:S(2)}) copy-start(f32[1024,64]{0,1:T(8,128)} %all-reduce.2.cloned.1.call-done) | copy-start | bytes 786436
Sparse Core Ops, SparseCore 0:
  86.7 34.0 all-reduce.1
  124.6 62.4 reduce-scatter.1
